TPU v7x, 128 devices: a whole 4x4x4 slice. The times are simulated.
128 devices in a mesh: fsdp: 32 (over y, x_hi, z), red: 4 (over x_lo, core).
Axes of the slice: x: 4 (x_hi: 2, x_lo: 2; x = x_hi * 2 + x_lo), y: 4, z: 4, core: 2. Of those that a mesh axis runs over, the one named last changes fastest.
Arguments:
- layer_input: bfloat16 [2, 8192, 16384], P(None, 'fsdp', 'red'), may hold values from -6 to 6
- kv_cotangent: bfloat16 [2, 8192, 1024], P(None, 'fsdp'), may hold values from -16 to 16
- failed_member: int32 [32], P('fsdp'), may hold values from 0 to 4
- master: float32 [2, 1024, 16384], P(None, 'fsdp', 'red'), may hold values from -0.046875 to 0.046875
- first_moment: float32 [2, 1024, 16384], P(None, 'fsdp', 'red'), may hold values from -4 to 4
- second_moment: float32 [2, 1024, 16384], P(None, 'fsdp', 'red'), may hold values from 0.05 to 2
- loss_scale: float32 [32, 4], P('fsdp', 'red'), may hold values from 2 to 8
- spare_master: float32 [2, 1024, 16384], P(None, 'fsdp', 'red'), may hold values from -0.046875 to 0.046875
- spare_first: float32 [2, 1024, 16384], P(None, 'fsdp', 'red'), may hold values from -4 to 4
- spare_second: float32 [2, 1024, 16384], P(None, 'fsdp', 'red'), may hold values from 0.05 to 2
- spare_scale: float32 [32, 4], P('fsdp', 'red'), may hold values from 2 to 8
Outputs:
- kv_out: bfloat16 [2, 8192, 1024], P(None, 'fsdp', 'red')
- input_grad: bfloat16 [2, 8192, 16384], P(None, 'fsdp', 'red')
- new_master: float32 [2, 1024, 16384], P(None, 'fsdp', 'red')
- new_first: float32 [2, 1024, 16384], P(None, 'fsdp', 'red')
- new_second: float32 [2, 1024, 16384], P(None, 'fsdp', 'red')
Inputs may be any that keep to these rules, and one draw needn't show every extreme that they name: failed_member[f] is the member of redundancy group f (index along red) whose state was lost; the value 4 means that group lost nothing.
All inputs are finite; a program needn't handle non-finite values.
Results may differ from a plain program's by a relative error of at most 0.017.
Values may be sent and summed in bfloat16 or wider, within the bound.
A program may use at most 128 MiB of HBM per device.

v0:
```python
import functools
import jax
import jax.numpy as jnp
from jax import lax
from jax.sharding import Mesh
from jax.sharding import PartitionSpec as P

RED = ("red_0", "red_1")
FSDP = ("fsdp_0", "fsdp_1", "fsdp_2")
FSDP_RED = ("fsdp_0", "fsdp_1", "fsdp_2", "red_0", "red_1")
BETA_FIRST = 0.9
BETA_SECOND = 0.95
LEARN_RATE = 0.01
DECAY_RATE = 0.1
ADAM_EPS = 1e-08
MEAN_EPS = 1e-06


def shifted(shard, axis, by):
    length = lax.axis_size(axis)
    return lax.ppermute(shard, axis, [(i, (i + by) % length) for i in range(length)])


def cut_along(shard, dim, length):
    before, after = (shard.shape[:dim], shard.shape[dim + 1 :])
    return jnp.moveaxis(shard.reshape(*before, length, -1, *after), dim, 0)


def sent_and_summed(shard, axis, dim):
    length = lax.axis_size(axis)
    parts = lax.all_to_all(cut_along(shard, dim, length), axis, 0, 0, tiled=True)
    return jnp.sum(parts.astype(jnp.float32), axis=0)


def reduced_to_own(parts, axes, order):
    inside = parts.shape[1:]
    parts = parts.reshape(*(lax.axis_size(a) for a in axes), *inside)
    parts = jnp.moveaxis(parts, order, range(len(axes))).reshape(-1, *inside)
    for k in order:
        parts = lax.psum_scatter(parts, axes[k], scatter_dimension=0, tiled=True)
    return parts[0]


def summed_rows(shard, axes, order, dim):
    length = lax.axis_size(axes)
    return reduced_to_own(cut_along(shard, dim, length), axes, order)


def by_axis(shard, axes):
    return functools.reduce(lax.psum, axes, shard)


def local(
    layer_input,
    kv_cotangent,
    failed_member,
    master,
    first_moment,
    second_moment,
    loss_scale,
    spare_master,
    spare_first,
    spare_second,
    spare_scale,
):
    layers = master.shape[0]
    local_rows = master.shape[1]
    replaced = lax.axis_index(RED) == failed_member[0]
    copy_master, copy_first, copy_second, copy_scale = (
        shifted(spare_master.astype(jnp.bfloat16), RED, 1).astype(spare_master.dtype),
        shifted(spare_first.astype(jnp.bfloat16), RED, 1).astype(spare_first.dtype),
        shifted(spare_second.astype(jnp.bfloat16), RED, 1).astype(spare_second.dtype),
        shifted(spare_scale.astype(jnp.bfloat16), RED, 1).astype(spare_scale.dtype),
    )
    master_now = jnp.where(replaced, copy_master, master)
    first_now = jnp.where(replaced, copy_first, first_moment)
    second_now = jnp.where(replaced, copy_second, second_moment)
    scale_now = jnp.where(replaced, copy_scale, loss_scale)
    weights = master_now.astype(jnp.bfloat16)
    gathered = lax.all_gather(weights, FSDP, axis=1, tiled=True)
    kv_list = []
    input_list = []
    for layer_index in range(layers):
        inputs = layer_input[layer_index]
        upstream = kv_cotangent[layer_index]
        full_weight = gathered[layer_index]
        partial_kv = lax.dot_general(
            inputs, full_weight, (((1,), (1,)), ((), ())), preferred_element_type=jnp.float32
        )
        kv_list.append(
            sent_and_summed(partial_kv.astype(jnp.bfloat16), RED, 1).astype(jnp.bfloat16)
        )
        input_list.append(
            jnp.dot(upstream, full_weight, preferred_element_type=jnp.float32).astype(jnp.bfloat16)
        )
    grad_terms = jnp.einsum(
        "ltc,ltd->lcd", kv_cotangent, layer_input, preferred_element_type=jnp.float32
    )
    grad_sum = summed_rows(grad_terms.astype(jnp.bfloat16), FSDP, (0, 2, 1), 1).astype(jnp.float32)
    gradient = grad_sum / scale_now[0, 0]
    total_squares = by_axis(jnp.sum(gradient * gradient), FSDP_RED)
    entries = layers * local_rows * lax.axis_size(FSDP) * master.shape[2] * lax.axis_size(RED)
    factor = jnp.minimum(1.0, lax.rsqrt(total_squares / entries + MEAN_EPS))
    clipped = gradient * factor
    new_first = BETA_FIRST * first_now + (1.0 - BETA_FIRST) * clipped
    new_second = BETA_SECOND * second_now + (1.0 - BETA_SECOND) * clipped * clipped
    new_master = master_now - LEARN_RATE * (
        new_first / (jnp.sqrt(new_second) + ADAM_EPS) + DECAY_RATE * master_now
    )
    return (jnp.stack(kv_list), jnp.stack(input_list), new_master, new_first, new_second)


def solution(mesh):
    split = Mesh(
        mesh.devices.reshape(4, 2, 4, 2, 2), ("fsdp_0", "fsdp_1", "fsdp_2", "red_0", "red_1")
    )
    placed = (
        P(None, FSDP, RED),
        P(None, FSDP, None),
        P(FSDP),
        P(None, FSDP, RED),
        P(None, FSDP, RED),
        P(None, FSDP, RED),
        P(FSDP, RED),
        P(None, FSDP, RED),
        P(None, FSDP, RED),
        P(None, FSDP, RED),
        P(FSDP, RED),
    )
    return jax.shard_map(
        local,
        mesh=split,
        in_specs=placed,
        out_specs=(
            P(None, FSDP, RED),
            P(None, FSDP, RED),
            P(None, FSDP, RED),
            P(None, FSDP, RED),
            P(None, FSDP, RED),
        ),
        check_vma=False,
    )
```

profile of v0, /device:TPU:1, one launch (start us, length us, event | category | flops | bytes accessed | tf_op | source)
XLA Modules:
  0.0 369.4 jit_solution(7072015989123471790)
XLA Ops:
  8.0 0.0 reduce-scatter.4.cloned.1.call-start
  8.0 12.8 %convolution_convert_fusion = bf16[2,1024,4096]{2,1,0:T(8,128)(2,1)} fusion(bf16[2,256,1024]{2,1,0:T(8,128)(2,1)} %param.12, bf16[2,256,4096]{2,1,0:T(8,128)(2,1)} %param.11), kind=kOutput, calls=%fused_computation | convolution fusion | flops 4303355904 | bytes 22020096 | tf_op jit(solution)/shard_map/ltc,ltd->lcd/dot_general | solution.py:96
  20.8 14.0 %copy.20 = bf16[4,2,4,2,32,4096]{5,4,3,1,2,0:T(8,128)(2,1)} copy(bf16[4,2,4,2,32,4096]{5,4,2,1,0,3:T(8,128)(2,1)} %bitcast.78) | data formatting | bytes 33554432 | tf_op jit(solution)/shard_map/reshape | solution.py:37
  34.8 0.0 copy-start.2
  34.8 0.0 copy-start
  34.8 0.0 reduce-scatter.4.cloned.1.call-update
  34.9 0.0 all-gather.2.cloned.1.call-start
  34.9 1.1 copy-done.2
  36.1 0.1 convert_element_type.62
  36.1 2.7 collective-permute-start
  39.4 0.0 copy-start.3
  39.4 5.5 %collective-permute-done = bf16[2,32,4096]{2,1,0:T(8,128)(2,1)S(1)} collective-permute-done((bf16[2,32,4096]{2,1,0:T(8,128)(2,1)S(1)}, bf16[2,32,4096]{2,1,0:T(8,128)(2,1)S(1)}, u32[]{:S(2)}, u32[]{:S(2)}) %collective-permute-start) | collective-permute-done | bytes 524320 | tf_op jit(solution)/shard_map/ppermute | solution.py:21
  44.9 0.0 copy-done
  44.9 0.9 fusion.20
  45.8 0.0 all-gather.2.cloned.1.call-update
  45.8 0.0 reduce-scatter.6.cloned.1.call-start
  45.9 179.6 %reduce-scatter.4.cloned.1.call-done = bf16[8,2,32,4096]{3,2,1,0:T(8,128)(2,1)} async-done(((bf16[32,2,32,4096]{3,2,1,0:T(8,128)(2,1)}), bf16[8,2,32,4096]{3,2,1,0:T(8,128)(2,1)}) %reduce-scatter.4.cloned.1.call-update) | async-done | bytes 4194320 | tf_op jit(solution)/shard_map/reduce_scatter | solution.py:40
  225.5 0.0 reduce-scatter.6.cloned.1.call-update
  226.2 2.9 collective-permute-start.2
  229.1 2.1 convert_element_type.73
  231.2 0.1 collective-permute-start.1
  231.3 0.0 copy-done.3
  231.3 0.8 convert_element_type.79
  232.1 0.6 collective-permute-start.3
  233.4 0.0 collective-permute-done.2
  234.0 13.6 %all-gather.2.cloned.1.call-done = bf16[2,1024,4096]{2,1,0:T(8,128)(2,1)} async-done(((bf16[2,32,4096]{2,1,0:T(8,128)(2,1)}), bf16[2,1024,4096]{2,1,0:T(8,128)(2,1)}) %all-gather.2.cloned.1.call-update) | async-done | bytes 16777232 | tf_op jit(solution)/shard_map/all_gather | solution.py:80
  247.6 7.3 %fusion.12 = bf16[1024,256]{1,0:T(8,128)(2,1)} fusion(bf16[2,256,4096]{2,1,0:T(8,128)(2,1)} %param.11, bf16[2,1024,4096]{2,1,0:T(8,128)(2,1)} %all-gather.2.cloned.1.call-done), kind=kOutput, calls=%fused_computation.17 | convolution fusion | flops 2147745792 | bytes 11010048 | tf_op jit(solution)/shard_map/dot_general | solution.py:87
  254.9 4.9 %all-to-all-start.1 = ((bf16[4,256,256]{1,2,0:T(8,128)(2,1)}), bf16[4,256,256]{1,2,0:T(8,128)(2,1)S(1)}, u32[]{:S(2)}, u32[]{:S(2)}) async-start(bf16[4,256,256]{1,2,0:T(8,128)(2,1)} %bitcast.11), calls=%async_computation.1 | async-start | bytes 1048576 | tf_op jit(solution)/shard_map/all_to_all | solution.py:31
  259.7 0.0 copy-start.4
  259.7 0.0 reduce-scatter.8.cloned.1.call-start
  259.7 7.3 %fusion.15 = bf16[1024,256]{1,0:T(8,128)(2,1)} fusion(bf16[2,256,4096]{2,1,0:T(8,128)(2,1)} %param.11, bf16[2,1024,4096]{2,1,0:T(8,128)(2,1)} %all-gather.2.cloned.1.call-done), kind=kOutput, calls=%fused_computation.18 | convolution fusion | flops 2147745792 | bytes 11010048 | tf_op jit(solution)/shard_map/dot_general | solution.py:87
  267.1 12.1 %reduce-scatter.6.cloned.1.call-done = bf16[2,2,32,4096]{3,2,1,0:T(8,128)(2,1)} async-done(((bf16[8,2,32,4096]{3,2,1,0:T(8,128)(2,1)}), bf16[2,2,32,4096]{3,2,1,0:T(8,128)(2,1)}) %reduce-scatter.6.cloned.1.call-update) | async-done | bytes 1048592 | tf_op jit(solution)/shard_map/reduce_scatter | solution.py:40
  279.1 0.0 reduce-scatter.8.cloned.1.call-update
  279.2 0.0 copy-done.4
  279.2 7.2 %fusion.6 = bf16[1,256,4096]{1,2,0:T(8,128)(2,1)} fusion(bf16[2,1024,4096]{2,1,0:T(8,128)(2,1)} %all-gather.2.cloned.1.call-done, bf16[2,256,1024]{2,1,0:T(8,128)(2,1)S(1)} %copy-done.4), kind=kOutput, calls=%fused_computation.9 | convolution fusion | flops 2148532224 | bytes 11010048 | tf_op jit(solution)/shard_map/dot_general | solution.py:94
  286.4 7.2 %fusion.7 = bf16[1,256,4096]{1,2,0:T(8,128)(2,1)} fusion(bf16[2,1024,4096]{2,1,0:T(8,128)(2,1)} %all-gather.2.cloned.1.call-done, bf16[2,256,1024]{2,1,0:T(8,128)(2,1)S(1)} %copy-done.4), kind=kOutput, calls=%fused_computation.10 | convolution fusion | flops 2148532224 | bytes 11010048 | tf_op jit(solution)/shard_map/dot_general | solution.py:94
  293.6 0.0 all-to-all-done.1
  293.6 5.0 %all-to-all-start = ((bf16[4,256,256]{1,2,0:T(8,128)(2,1)}), bf16[4,256,256]{1,2,0:T(8,128)(2,1)S(1)}, u32[]{:S(2)}, u32[]{:S(2)}) async-start(bf16[4,256,256]{1,2,0:T(8,128)(2,1)} %bitcast.79), calls=%async_computation | async-start | bytes 1048576 | tf_op jit(solution)/shard_map/all_to_all | solution.py:31
  298.7 4.6 %pad_maximum_fusion = bf16[2,256,4096]{1,2,0:T(8,128)(2,1)} fusion(bf16[1,256,4096]{1,2,0:T(8,128)(2,1)} %fusion.7, bf16[1,256,4096]{1,2,0:T(8,128)(2,1)} %fusion.6), kind=kLoop, calls=%fused_computation.11 | loop fusion | flops 2097152 | bytes 8388608 | tf_op jit(solution)/shard_map/stack | solution.py:110
  303.2 4.0 %reduce-scatter.8.cloned.1.call-done = bf16[1,2,32,4096]{3,2,1,0:T(8,128)(2,1)} async-done(((bf16[2,2,32,4096]{3,2,1,0:T(8,128)(2,1)}), bf16[1,2,32,4096]{3,2,1,0:T(8,128)(2,1)}) %reduce-scatter.8.cloned.1.call-update) | async-done | bytes 524304 | tf_op jit(solution)/shard_map/reduce_scatter | solution.py:40
  307.2 1.9 multiply_reduce_fusion
  309.1 0.0 copy-start.1
  309.1 6.4 %copy.22 = bf16[2,256,4096]{2,1,0:T(8,128)(2,1)} copy(bf16[2,256,4096]{1,2,0:T(8,128)(2,1)} %pad_maximum_fusion) | data formatting | bytes 8388608
  315.5 9.1 %psum.35 = f32[]{:T(128)} all-reduce(f32[]{:T(128)} %multiply_reduce_fusion), channel_id=1, replica_groups=mesh['fsdp_0'=4,'fsdp_1'=2,'fsdp_2'=4,'red_0'=2,'red_1'=2] {'fsdp_0'}, use_global_device_ids=true, to_apply=%region_6.7 | all-reduce | flops 1 | bytes 8 | tf_op jit(solution)/shard_map/psum | solution.py:50
  324.6 0.1 reduce_sum.34
  324.6 5.9 %psum.36 = f32[]{:T(128)} all-reduce(f32[]{:T(128)} %psum.35), channel_id=1, replica_groups=mesh['fsdp_0'=4,'fsdp_1'=2,'fsdp_2'=4,'red_0'=2,'red_1'=2] {'fsdp_1'}, use_global_device_ids=true, to_apply=%region_7.8 | all-reduce | flops 1 | bytes 8 | tf_op jit(solution)/shard_map/psum | solution.py:50
  330.6 0.0 all-to-all-done
  330.6 0.1 reduce_sum.33
  330.6 11.5 %psum.37 = f32[]{:T(128)} all-reduce(f32[]{:T(128)} %psum.36), channel_id=1, replica_groups=mesh['fsdp_0'=4,'fsdp_1'=2,'fsdp_2'=4,'red_0'=2,'red_1'=2] {'fsdp_2'}, use_global_device_ids=true, to_apply=%region_8.9 | all-reduce | flops 1 | bytes 8 | tf_op jit(solution)/shard_map/psum | solution.py:50
  342.2 4.4 %psum.38 = f32[]{:T(128)} all-reduce(f32[]{:T(128)} %psum.37), channel_id=1, replica_groups=mesh['fsdp_0'=4,'fsdp_1'=2,'fsdp_2'=4,'red_0'=2,'red_1'=2] {'red_0'}, use_global_device_ids=true, to_apply=%region_9.10 | all-reduce | flops 1 | bytes 8 | tf_op jit(solution)/shard_map/psum | solution.py:50
  346.6 0.8 copy.21
  347.4 10.6 %psum.39 = f32[]{:T(128)} all-reduce(f32[]{:T(128)} %psum.38), channel_id=1, replica_groups=mesh['fsdp_0'=4,'fsdp_1'=2,'fsdp_2'=4,'red_0'=2,'red_1'=2] {'red_1'}, use_global_device_ids=true, to_apply=%region_10.11 | all-reduce | flops 1 | bytes 8 | tf_op jit(solution)/shard_map/psum | solution.py:50
  358.7 0.0 collective-permute-done.1
  358.7 0.0 collective-permute-done.3
  358.7 0.0 copy-done.1
  358.7 3.5 multiply_subtract_fusion
  (1 shorter events, 0.0 us)
Async XLA Ops:
  8.0 217.5 %reduce-scatter.4.cloned.1.call-start = ((), (), s32[]{:S(2)}) async-start(), calls=%async_computation.6 | async-start | bytes 20971520 | tf_op jit(solution)/shard_map/reduce_scatter | solution.py:40
  34.8 1.2 copy-start.2
  34.8 10.1 %copy-start = (f32[2,32,4096]{2,1,0:T(8,128)S(1)}, f32[2,32,4096]{2,1,0:T(8,128)}, u32[]{:S(2)}) copy-start(f32[2,32,4096]{2,1,0:T(8,128)} %param.14) | copy-start | bytes 3145732
  34.9 212.7 %all-gather.2.cloned.1.call-start = ((), (), s32[]{:S(2)}) async-start(), calls=%async_computation.5 | async-start | bytes 17301504 | tf_op jit(solution)/shard_map/all_gather | solution.py:80
  36.1 8.8 %collective-permute-start = (bf16[2,32,4096]{2,1,0:T(8,128)(2,1)S(1)}, bf16[2,32,4096]{2,1,0:T(8,128)(2,1)S(1)}, u32[]{:S(2)}, u32[]{:S(2)}) collective-permute-start(bf16[2,32,4096]{2,1,0:T(8,128)(2,1)S(1)} %convert_element_type.62), channel_id=1, source_target_pairs={{0,1},{1,2},{2,3},{3,0},{4,5},{5,6},{6,7},{7,4},{8,9},{9,10},{10,1... | collective-permute-start | bytes 1572872 | tf_op jit(solution)/shard_map/ppermute | solution.py:21
  39.4 191.9 %copy-start.3 = (f32[2,32,4096]{2,1,0:T(8,128)S(1)}, f32[2,32,4096]{2,1,0:T(8,128)}, u32[]{:S(2)}) copy-start(f32[2,32,4096]{2,1,0:T(8,128)} %param.20) | copy-start | bytes 3145732
  45.8 233.3 %reduce-scatter.6.cloned.1.call-start = ((), (), s32[]{:S(2)}) async-start(), calls=%async_computation.7 | async-start | bytes 5242880 | tf_op jit(solution)/shard_map/reduce_scatter | solution.py:40
  226.2 7.2 %collective-permute-start.2 = (bf16[1,1]{1,0:T(2,128)(2,1)}, bf16[1,1]{1,0:T(2,128)(2,1)}, u32[]{:S(2)}, u32[]{:S(2)}) collective-permute-start(bf16[1,1]{1,0:T(2,128)(2,1)} %convert_element_type.77), channel_id=1, source_target_pairs={{0,1},{1,2},{2,3},{3,0},{4,5},{5,6},{6,7},{7,4},{8,9},{9,10},{10,1... | collective-permute-start | bytes 14 | tf_op jit(solution)/shard_map/ppermute | solution.py:21
  231.2 127.5 %collective-permute-start.1 = (bf16[2,32,4096]{2,1,0:T(8,128)(2,1)}, bf16[2,32,4096]{2,1,0:T(8,128)(2,1)}, u32[]{:S(2)}, u32[]{:S(2)}) collective-permute-start(bf16[2,32,4096]{2,1,0:T(8,128)(2,1)} %convert_element_type.73), channel_id=1, source_target_pairs={{0,1},{1,2},{2,3},{3,0},{4,5},{5,6},{6,7},{7,4},{8,9},{9,10},{10,1... | collective-permute-start | bytes 1572872 | tf_op jit(solution)/shard_map/ppermute | solution.py:21
  232.1 126.6 %collective-permute-start.3 = (bf16[2,32,4096]{2,1,0:T(8,128)(2,1)}, bf16[2,32,4096]{2,1,0:T(8,128)(2,1)}, u32[]{:S(2)}, u32[]{:S(2)}) collective-permute-start(bf16[2,32,4096]{2,1,0:T(8,128)(2,1)} %convert_element_type.79), channel_id=1, source_target_pairs={{0,1},{1,2},{2,3},{3,0},{4,5},{5,6},{6,7},{7,4},{8,9},{9,10},{10,1... | collective-permute-start | bytes 1572872 | tf_op jit(solution)/shard_map/ppermute | solution.py:21
  254.9 38.8 %all-to-all-start.1 = ((bf16[4,256,256]{1,2,0:T(8,128)(2,1)}), bf16[4,256,256]{1,2,0:T(8,128)(2,1)S(1)}, u32[]{:S(2)}, u32[]{:S(2)}) async-start(bf16[4,256,256]{1,2,0:T(8,128)(2,1)} %bitcast.11), calls=%async_computation.1 | async-start | bytes 1048576 | tf_op jit(solution)/shard_map/all_to_all | solution.py:31
  259.7 19.4 %copy-start.4 = (bf16[2,256,1024]{2,1,0:T(8,128)(2,1)S(1)}, bf16[2,256,1024]{2,1,0:T(8,128)(2,1)}, u32[]{:S(2)}) copy-start(bf16[2,256,1024]{2,1,0:T(8,128)(2,1)} %param.12) | copy-start | bytes 3145732
  259.7 47.5 %reduce-scatter.8.cloned.1.call-start = ((), (), s32[]{:S(2)}) async-start(), calls=%async_computation.8 | async-start | bytes 1572864 | tf_op jit(solution)/shard_map/reduce_scatter | solution.py:40
  293.6 36.9 %all-to-all-start = ((bf16[4,256,256]{1,2,0:T(8,128)(2,1)}), bf16[4,256,256]{1,2,0:T(8,128)(2,1)S(1)}, u32[]{:S(2)}, u32[]{:S(2)}) async-start(bf16[4,256,256]{1,2,0:T(8,128)(2,1)} %bitcast.79), calls=%async_computation | async-start | bytes 1048576 | tf_op jit(solution)/shard_map/all_to_all | solution.py:31
  309.1 49.6 %copy-start.1 = (bf16[1,2,32,4096]{3,2,1,0:T(8,128)(2,1)S(1)}, bf16[1,2,32,4096]{3,2,1,0:T(8,128)(2,1)}, u32[]{:S(2)}) copy-start(bf16[1,2,32,4096]{3,2,1,0:T(8,128)(2,1)} %reduce-scatter.8.cloned.1.call-done) | copy-start | bytes 1572868
Sparse Core Ops, SparseCore 0:
  35.0 190.4 reduce-scatter.3
  227.9 51.1 reduce-scatter.5
  281.5 25.6 reduce-scatter.7
Sparse Core Ops, SparseCore 1:
  45.9 201.7 all-gather.1
where the time goes:
time: 370 us; the launch traced here: 369 us
  waiting for transfers between devices  215 us (58%)
  matrix products  41.8 us (11%)
  blocking collectives  41.5 us (11%)
  local copies, waits for them, and re-layouts  22.4 us (6%)
  between operations  18.5 us (5%)
  starting transfers between devices  16.3 us (4%)
  other arithmetic  14.1 us (4%)
    reduce_scatter x3, waiting for transfers between devices, reduced_to_own(): parts = lax.psum_scatter(parts, axes[k], scatter_dimension=0, tiled=True)  196 us
    psum x5, blocking collectives, by_axis(): return functools.reduce(lax.psum, axes, shard)  41.5 us
    dot_general x2, matrix products, local(): lax.dot_general(inputs, full_weight, (((1,), (1,)), ((), ())), preferred_...  14.6 us
    dot_general x2, matrix products, local(): jnp.dot(upstream, full_weight, preferred_element_type=jnp.float32)  14.5 us
    reshape x1, local copies, waits for them, and re-layouts, reduced_to_own(): parts = parts.reshape(*(lax.axis_size(a) for a in axes), *inside)  14 us
    all_gather x1, waiting for transfers between devices, local(): gathered = lax.all_gather(weights, FSDP, axis=1, tiled=True)  13.6 us
    dot_general x1, matrix products, local(): jnp.einsum('ltc,ltd->lcd', kv_cotangent, layer_input, preferred_element_t...  12.8 us
    all_to_all x2, starting transfers between devices, sent_and_summed(): lax.all_to_all(cut_along(shard, dim, length), axis, 0, 0, tiled=True)  9.91 us
  transfers between devices with their start and end apart: 10, of which 5 were waited for; matrix products, arithmetic and copies ran while one was open for 13% of the time, Pallas kernels for 0%

commit v1 on v0

--- a/solution.py
+++ b/solution.py
@@ -77,7 +77,9 @@
     second_now = jnp.where(replaced, copy_second, second_moment)
     scale_now = jnp.where(replaced, copy_scale, loss_scale)
     weights = master_now.astype(jnp.bfloat16)
-    gathered = lax.all_gather(weights, FSDP, axis=1, tiled=True)
+    gathered = jnp.concatenate(
+        lax.all_to_all(jnp.stack([weights] * lax.axis_size(FSDP)), FSDP, 0, 0), axis=1
+    )
     kv_list = []
     input_list = []
     for layer_index in range(layers):

time: 370 us -> 546 us (1.48)
  waiting for transfers between devices: 215 us -> 372 us
  local copies, waits for them, and re-layouts: 22.4 us -> 41.6 us
  starting transfers between devices: 16.3 us -> 27 us
  blocking collectives: 41.5 us -> 35.7 us
    reduce_scatter x3, waiting for transfers between devices: 196 us -> 367 us  [reduced_to_own(): parts = lax.psum_scatter(parts, axes[k], scatter_dimension=0, tiled=True)]
    all_gather x1 -> x0, waiting for transfers between devices: 13.6 us -> none  [local(): gathered = lax.all_gather(weights, FSDP, axis=1, tiled=True)]
    all_to_all x0 -> x1, starting transfers between devices: none -> 10.4 us  [local(): lax.all_to_all(jnp.stack([weights] * lax.axis_size(FSDP)), FSDP, 0, 0)]
    slice x0 -> x1, local copies, waits for them, and re-layouts: none -> 9.62 us  [local(): full_weight = gathered[layer_index]]
    another operation x0 -> x1, local copies, waits for them, and re-layouts: none -> 6.26 us  [local(): jnp.stack([weights] * lax.axis_size(FSDP))]
    psum x5, blocking collectives: 41.5 us -> 35.7 us  [by_axis(): return functools.reduce(lax.psum, axes, shard)]
    unnamed x12 -> x18, local copies, waits for them, and re-layouts: 8.38 us -> 11.7 us
  transfers between devices with their start and end apart: 10 -> 10, of which waited for: 5 -> 3; matrix products, arithmetic and copies ran while one was open for 13% -> 11% of each run, Pallas kernels for 0% -> 0%
where the time goes in v1:
time: 546 us; the launch traced here: 545 us
  waiting for transfers between devices  372 us (68%)
  local copies, waits for them, and re-layouts  41.6 us (8%)
  matrix products  37.6 us (7%)
  blocking collectives  35.7 us (7%)
  starting transfers between devices  27 us (5%)
  between operations  17.1 us (3%)
  other arithmetic  13.3 us (2%)
    reduce_scatter x3, waiting for transfers between devices, reduced_to_own(): parts = lax.psum_scatter(parts, axes[k], scatter_dimension=0, tiled=True)  367 us
    psum x5, blocking collectives, by_axis(): return functools.reduce(lax.psum, axes, shard)  35.7 us
    dot_general x2, matrix products, local(): jnp.dot(upstream, full_weight, preferred_element_type=jnp.float32)  14.5 us
    reshape x1, local copies, waits for them, and re-layouts, reduced_to_own(): parts = parts.reshape(*(lax.axis_size(a) for a in axes), *inside)  14 us
    dot_general x1, matrix products, local(): jnp.einsum('ltc,ltd->lcd', kv_cotangent, layer_input, preferred_element_t...  12.8 us
    unnamed x18, local copies, waits for them, and re-layouts  11.7 us
  transfers between devices with their start and end apart: 10, of which 3 were waited for; matrix products, arithmetic and copies ran while one was open for 11% of the time, Pallas kernels for 0%

profile of v1, /device:TPU:1, one launch (start us, length us, event | category | flops | bytes accessed | tf_op | source)
XLA Modules:
  0.0 544.6 jit_solution(18169683267736046456)
XLA Ops:
  7.2 0.0 reduce-scatter.4.cloned.1.call-start
  7.2 12.8 %convolution_convert_fusion = bf16[2,1024,4096]{2,1,0:T(8,128)(2,1)} fusion(bf16[2,256,1024]{2,1,0:T(8,128)(2,1)} %param.12, bf16[2,256,4096]{2,1,0:T(8,128)(2,1)} %param.11), kind=kOutput, calls=%fused_computation | convolution fusion | flops 4303355904 | bytes 22020096 | tf_op jit(solution)/shard_map/ltc,ltd->lcd/dot_general | solution.py:98
  20.0 14.0 %copy.20 = bf16[4,2,4,2,32,4096]{5,4,3,1,2,0:T(8,128)(2,1)} copy(bf16[4,2,4,2,32,4096]{5,4,2,1,0,3:T(8,128)(2,1)} %bitcast.65) | data formatting | bytes 33554432 | tf_op jit(solution)/shard_map/reshape | solution.py:37
  34.0 0.0 copy-start.4
  34.0 0.0 copy-start.1
  34.0 0.0 reduce-scatter.4.cloned.1.call-update
  34.0 1.2 copy-done.4
  35.2 0.1 convert_element_type.62
  35.3 2.7 collective-permute-start
  38.6 5.5 %collective-permute-done = bf16[2,32,4096]{2,1,0:T(8,128)(2,1)S(1)} collective-permute-done((bf16[2,32,4096]{2,1,0:T(8,128)(2,1)S(1)}, bf16[2,32,4096]{2,1,0:T(8,128)(2,1)S(1)}, u32[]{:S(2)}, u32[]{:S(2)}) %collective-permute-start) | collective-permute-done | bytes 524320 | tf_op jit(solution)/shard_map/ppermute | solution.py:21
  44.1 0.0 copy-done.1
  44.1 0.1 fusion.16
  44.2 6.3 %stack.14 = bf16[32,2,32,4096]{3,2,1,0:T(8,128)(2,1)} broadcast(bf16[2,32,4096]{2,1,0:T(8,128)(2,1)S(1)} %fusion.16), dimensions={1,2,3} | broadcast | bytes 17301504 | tf_op jit(solution)/shard_map/stack | solution.py:81
  50.4 10.4 %all-to-all-start = ((bf16[32,2,32,4096]{3,2,1,0:T(8,128)(2,1)}), bf16[32,2,32,4096]{3,2,1,0:T(8,128)(2,1)}, u32[]{:S(2)}, u32[]{:S(2)}) async-start(bf16[32,2,32,4096]{3,2,1,0:T(8,128)(2,1)} %stack.14), calls=%async_computation | async-start | bytes 33554432 | tf_op jit(solution)/shard_map/all_to_all | solution.py:81
  60.8 0.0 copy-start.5
  60.8 0.0 reduce-scatter.6.cloned.1.call-start
  60.9 327.1 %reduce-scatter.4.cloned.1.call-done = bf16[8,2,32,4096]{3,2,1,0:T(8,128)(2,1)} async-done(((bf16[32,2,32,4096]{3,2,1,0:T(8,128)(2,1)}), bf16[8,2,32,4096]{3,2,1,0:T(8,128)(2,1)}) %reduce-scatter.4.cloned.1.call-update) | async-done | bytes 4194320 | tf_op jit(solution)/shard_map/reduce_scatter | solution.py:40
  388.0 0.0 reduce-scatter.6.cloned.1.call-update
  388.0 0.0 reduce-scatter.8.cloned.1.call-start
  388.7 5.7 %collective-permute-start.2 = (bf16[1,1]{1,0:T(2,128)(2,1)}, bf16[1,1]{1,0:T(2,128)(2,1)}, u32[]{:S(2)}, u32[]{:S(2)}) collective-permute-start(bf16[1,1]{1,0:T(2,128)(2,1)} %convert_element_type.77), channel_id=1, source_target_pairs={{0,1},{1,2},{2,3},{3,0},{4,5},{5,6},{6,7},{7,4},{8,9},{9,10},{10,1... | collective-permute-start | bytes 14 | tf_op jit(solution)/shard_map/ppermute | solution.py:21
  394.4 0.0 copy-done.5
  394.4 0.9 convert_element_type.73
  395.3 0.1 collective-permute-start.1
  395.4 2.1 convert_element_type.79
  397.5 0.0 collective-permute-start.3
  398.1 0.0 collective-permute-done.2
  398.8 0.0 all-to-all-done
  398.8 0.0 copy-start.2
  398.8 9.6 %fusion.23 = (bf16[1,32,32,4096]{3,2,0,1:T(8,128)(2,1)}, bf16[1,32,32,4096]{3,2,0,1:T(8,128)(2,1)S(1)}) fusion(bf16[2,32,32,4096]{3,2,0,1:T(8,128)(2,1)} %bitcast.1), kind=kLoop, calls=%fused_computation.28 | loop fusion | bytes 33554432 | tf_op jit(solution)/shard_map/slice | solution.py:88
  408.4 0.0 copy-start
  408.4 3.2 copy-done
  411.6 0.0 copy-done.2
  411.6 0.0 copy-start.6
  411.7 3.2 fusion.11
  414.8 39.6 %reduce-scatter.6.cloned.1.call-done = bf16[2,2,32,4096]{3,2,1,0:T(8,128)(2,1)} async-done(((bf16[8,2,32,4096]{3,2,1,0:T(8,128)(2,1)}), bf16[2,2,32,4096]{3,2,1,0:T(8,128)(2,1)}) %reduce-scatter.6.cloned.1.call-update) | async-done | bytes 1048592 | tf_op jit(solution)/shard_map/reduce_scatter | solution.py:40
  454.5 0.0 reduce-scatter.8.cloned.1.call-update
  454.5 0.0 copy-done.6
  454.5 7.3 %fusion = bf16[1,256,4096]{1,2,0:T(8,128)(2,1)} fusion(bf16[1024,4096]{1,0:T(8,128)(2,1)} %bitcast.68, bf16[2,256,1024]{2,1,0:T(8,128)(2,1)S(1)} %copy-done.6), kind=kOutput, calls=%fused_computation.3 | convolution fusion | flops 2148532224 | bytes 11010048 | tf_op jit(solution)/shard_map/dot_general | solution.py:96
  461.8 4.2 all-to-all-start.2
  465.9 0.0 copy-start.7
  466.0 7.2 %fusion.8 = bf16[1024,256]{1,0:T(8,128)(2,1)} fusion(bf16[1024,4096]{1,0:T(8,128)(2,1)} %bitcast.69, bf16[2,256,4096]{2,1,0:T(8,128)(2,1)} %param.11), kind=kOutput, calls=%fused_computation.13 | convolution fusion | flops 2147745792 | bytes 11010048 | tf_op jit(solution)/shard_map/dot_general | solution.py:89
  473.2 0.0 copy-done.7
  473.2 7.2 %fusion.1 = bf16[1,256,4096]{1,2,0:T(8,128)(2,1)} fusion(bf16[1024,4096]{1,0:T(8,128)(2,1)} %bitcast.67, bf16[2,256,1024]{2,1,0:T(8,128)(2,1)S(1)} %copy-done.7), kind=kOutput, calls=%fused_computation.4 | convolution fusion | flops 2148532224 | bytes 11010048 | tf_op jit(solution)/shard_map/dot_general | solution.py:96
  480.4 0.0 all-to-all-done.2
  480.4 3.8 all-to-all-start.1
  484.2 4.5 pad_maximum_fusion
  488.7 0.0 reduce-scatter.8.cloned.1.call-done
  488.7 1.9 multiply_reduce_fusion
  490.7 0.0 copy-start.3
  490.7 6.4 %copy.22 = bf16[2,256,4096]{2,1,0:T(8,128)(2,1)} copy(bf16[2,256,4096]{1,2,0:T(8,128)(2,1)} %pad_maximum_fusion) | data formatting | bytes 8388608
  497.0 9.1 %psum.35 = f32[]{:T(128)} all-reduce(f32[]{:T(128)} %multiply_reduce_fusion), channel_id=1, replica_groups=mesh['fsdp_0'=4,'fsdp_1'=2,'fsdp_2'=4,'red_0'=2,'red_1'=2] {'fsdp_0'}, use_global_device_ids=true, to_apply=%region_6.7 | all-reduce | flops 1 | bytes 8 | tf_op jit(solution)/shard_map/psum | solution.py:50
  506.1 0.1 reduce_sum.34
  506.2 5.9 %psum.36 = f32[]{:T(128)} all-reduce(f32[]{:T(128)} %psum.35), channel_id=1, replica_groups=mesh['fsdp_0'=4,'fsdp_1'=2,'fsdp_2'=4,'red_0'=2,'red_1'=2] {'fsdp_1'}, use_global_device_ids=true, to_apply=%region_7.8 | all-reduce | flops 1 | bytes 8 | tf_op jit(solution)/shard_map/psum | solution.py:50
  512.1 0.0 all-to-all-done.1
  512.1 0.1 reduce_sum.33
  512.2 7.2 %psum.37 = f32[]{:T(128)} all-reduce(f32[]{:T(128)} %psum.36), channel_id=1, replica_groups=mesh['fsdp_0'=4,'fsdp_1'=2,'fsdp_2'=4,'red_0'=2,'red_1'=2] {'fsdp_2'}, use_global_device_ids=true, to_apply=%region_8.9 | all-reduce | flops 1 | bytes 8 | tf_op jit(solution)/shard_map/psum | solution.py:50
  519.4 4.7 psum.38
  524.1 0.8 copy.21
  525.0 8.8 %psum.39 = f32[]{:T(128)} all-reduce(f32[]{:T(128)} %psum.38), channel_id=1, replica_groups=mesh['fsdp_0'=4,'fsdp_1'=2,'fsdp_2'=4,'red_0'=2,'red_1'=2] {'red_1'}, use_global_device_ids=true, to_apply=%region_10.11 | all-reduce | flops 1 | bytes 8 | tf_op jit(solution)/shard_map/psum | solution.py:50
  534.5 0.0 collective-permute-done.1
  534.5 0.0 collective-permute-done.3
  534.5 0.0 copy-done.3
  534.5 3.5 multiply_subtract_fusion
  (1 shorter events, 0.0 us)
Async XLA Ops:
  7.2 380.8 %reduce-scatter.4.cloned.1.call-start = ((), (), s32[]{:S(2)}) async-start(), calls=%async_computation.6 | async-start | bytes 20971520 | tf_op jit(solution)/shard_map/reduce_scatter | solution.py:40
  34.0 1.2 copy-start.4
  34.0 10.1 %copy-start.1 = (f32[2,32,4096]{2,1,0:T(8,128)S(1)}, f32[2,32,4096]{2,1,0:T(8,128)}, u32[]{:S(2)}) copy-start(f32[2,32,4096]{2,1,0:T(8,128)} %param.14) | copy-start | bytes 3145732
  35.3 8.8 %collective-permute-start = (bf16[2,32,4096]{2,1,0:T(8,128)(2,1)S(1)}, bf16[2,32,4096]{2,1,0:T(8,128)(2,1)S(1)}, u32[]{:S(2)}, u32[]{:S(2)}) collective-permute-start(bf16[2,32,4096]{2,1,0:T(8,128)(2,1)S(1)} %convert_element_type.62), channel_id=1, source_target_pairs={{0,1},{1,2},{2,3},{3,0},{4,5},{5,6},{6,7},{7,4},{8,9},{9,10},{10,1... | collective-permute-start | bytes 1572872 | tf_op jit(solution)/shard_map/ppermute | solution.py:21
  50.4 348.4 %all-to-all-start = ((bf16[32,2,32,4096]{3,2,1,0:T(8,128)(2,1)}), bf16[32,2,32,4096]{3,2,1,0:T(8,128)(2,1)}, u32[]{:S(2)}, u32[]{:S(2)}) async-start(bf16[32,2,32,4096]{3,2,1,0:T(8,128)(2,1)} %stack.14), calls=%async_computation | async-start | bytes 33554432 | tf_op jit(solution)/shard_map/all_to_all | solution.py:81
  60.8 333.6 %copy-start.5 = (f32[2,32,4096]{2,1,0:T(8,128)S(1)}, f32[2,32,4096]{2,1,0:T(8,128)}, u32[]{:S(2)}) copy-start(f32[2,32,4096]{2,1,0:T(8,128)} %param.19) | copy-start | bytes 3145732
  60.8 393.6 %reduce-scatter.6.cloned.1.call-start = ((), (), s32[]{:S(2)}) async-start(), calls=%async_computation.7 | async-start | bytes 5242880 | tf_op jit(solution)/shard_map/reduce_scatter | solution.py:40
  388.0 100.7 %reduce-scatter.8.cloned.1.call-start = ((), (), s32[]{:S(2)}) async-start(), calls=%async_computation.8 | async-start | bytes 1572864 | tf_op jit(solution)/shard_map/reduce_scatter | solution.py:40
  388.7 9.4 %collective-permute-start.2 = (bf16[1,1]{1,0:T(2,128)(2,1)}, bf16[1,1]{1,0:T(2,128)(2,1)}, u32[]{:S(2)}, u32[]{:S(2)}) collective-permute-start(bf16[1,1]{1,0:T(2,128)(2,1)} %convert_element_type.77), channel_id=1, source_target_pairs={{0,1},{1,2},{2,3},{3,0},{4,5},{5,6},{6,7},{7,4},{8,9},{9,10},{10,1... | collective-permute-start | bytes 14 | tf_op jit(solution)/shard_map/ppermute | solution.py:21
  395.3 139.2 %collective-permute-start.1 = (bf16[2,32,4096]{2,1,0:T(8,128)(2,1)}, bf16[2,32,4096]{2,1,0:T(8,128)(2,1)}, u32[]{:S(2)}, u32[]{:S(2)}) collective-permute-start(bf16[2,32,4096]{2,1,0:T(8,128)(2,1)} %convert_element_type.73), channel_id=1, source_target_pairs={{0,1},{1,2},{2,3},{3,0},{4,5},{5,6},{6,7},{7,4},{8,9},{9,10},{10,1... | collective-permute-start | bytes 1572872 | tf_op jit(solution)/shard_map/ppermute | solution.py:21
  397.5 137.0 %collective-permute-start.3 = (bf16[2,32,4096]{2,1,0:T(8,128)(2,1)}, bf16[2,32,4096]{2,1,0:T(8,128)(2,1)}, u32[]{:S(2)}, u32[]{:S(2)}) collective-permute-start(bf16[2,32,4096]{2,1,0:T(8,128)(2,1)} %convert_element_type.79), channel_id=1, source_target_pairs={{0,1},{1,2},{2,3},{3,0},{4,5},{5,6},{6,7},{7,4},{8,9},{9,10},{10,1... | collective-permute-start | bytes 1572872 | tf_op jit(solution)/shard_map/ppermute | solution.py:21
  398.8 12.9 %copy-start.2 = (bf16[2,256,4096]{2,1,0:T(8,128)(2,1)S(1)}, bf16[2,256,4096]{2,1,0:T(8,128)(2,1)}, u32[]{:S(2)}) copy-start(bf16[2,256,4096]{2,1,0:T(8,128)(2,1)} %param.11) | copy-start | bytes 12582916
  408.4 3.2 copy-start
  411.6 42.8 %copy-start.6 = (bf16[2,256,1024]{2,1,0:T(8,128)(2,1)S(1)}, bf16[2,256,1024]{2,1,0:T(8,128)(2,1)}, u32[]{:S(2)}) copy-start(bf16[2,256,1024]{2,1,0:T(8,128)(2,1)} %param.12) | copy-start | bytes 3145732
  461.8 18.6 %all-to-all-start.2 = ((bf16[4,256,256]{1,2,0:T(8,128)(2,1)}), bf16[4,256,256]{1,2,0:T(8,128)(2,1)S(1)}, u32[]{:S(2)}, u32[]{:S(2)}) async-start(bf16[4,256,256]{1,2,0:T(8,128)(2,1)} %bitcast.12), calls=%async_computation.2 | async-start | bytes 1048576 | tf_op jit(solution)/shard_map/all_to_all | solution.py:31
  465.9 7.2 %copy-start.7 = (bf16[2,256,1024]{2,1,0:T(8,128)(2,1)S(1)}, bf16[2,256,1024]{2,1,0:T(8,128)(2,1)}, u32[]{:S(2)}) copy-start(bf16[2,256,1024]{2,1,0:T(8,128)(2,1)} %param.12) | copy-start | bytes 3145732
  480.4 31.7 %all-to-all-start.1 = ((bf16[4,256,256]{1,2,0:T(8,128)(2,1)}), bf16[4,256,256]{1,2,0:T(8,128)(2,1)S(1)}, u32[]{:S(2)}, u32[]{:S(2)}) async-start(bf16[4,256,256]{1,2,0:T(8,128)(2,1)} %bitcast.6), calls=%async_computation.1 | async-start | bytes 1048576 | tf_op jit(solution)/shard_map/all_to_all | solution.py:31
  490.7 43.9 %copy-start.3 = (bf16[1,2,32,4096]{3,2,1,0:T(8,128)(2,1)S(1)}, bf16[1,2,32,4096]{3,2,1,0:T(8,128)(2,1)}, u32[]{:S(2)}) copy-start(bf16[1,2,32,4096]{3,2,1,0:T(8,128)(2,1)} %reduce-scatter.8.cloned.1.call-done) | copy-start | bytes 1572868
Sparse Core Ops, SparseCore 0:
  34.1 353.7 reduce-scatter.3
  390.4 64.0 reduce-scatter.5
  456.8 29.4 reduce-scatter.7
